TPU v7x, 32 devices: a whole 2x2x4 slice. The times are simulated.
32 devices in a mesh: groups: 2 (over x), tok: 16 (over z, y, core).
Axes of the slice: x: 2, y: 2, z: 4, core: 2. Of those that a mesh axis runs over, the one named last changes fastest.
Arguments:
- queries: bfloat16 [4096, 2048], P(('groups', 'tok')), parts along dimension 0, may hold values from -6 to 6
- key_matrix: bfloat16 [4096, 512], P(('groups', 'tok')), parts along dimension 0, may hold values from -6 to 6
- value_matrix: bfloat16 [4096, 512], P(('groups', 'tok')), parts along dimension 0, may hold values from -6 to 6
- attention_output: bfloat16 [4096, 2048], P(('groups', 'tok')), parts along dimension 0, may hold values from -3 to 3
- output_gradient: bfloat16 [4096, 2048], P(('groups', 'tok')), parts along dimension 0, may hold values from -48 to 48
- log_sum_norm: float32 [16, 4096], P(None, ('groups', 'tok')), parts along dimension 1, may hold values from 6 to 8
- doc_ids: int32 [4096], P(('groups', 'tok')), parts along dimension 0, may hold values from 0 to 7, never falling along the last dimension, each value on 1 to 1024 neighbouring positions
Outputs:
- query_grad: bfloat16 [4096, 2048], P(('groups', 'tok')), parts along dimension 0
- key_grad: bfloat16 [4096, 512], P(('groups', 'tok')), parts along dimension 0
- value_grad: bfloat16 [4096, 512], P(('groups', 'tok')), parts along dimension 0
There are 2 independent parts, one for each index of `groups`. A program takes and returns all parts, laid end to end along the dimension named above; each array names one. Nothing has to cross between parts.
Inputs may be any that keep to these rules, and one draw needn't show every extreme that they name: `doc_ids`: document ids never fall along the slab; each document has 1 to 1024 tokens and one has exactly 1024.
All inputs are finite; a program needn't handle non-finite values.
Results may differ from a plain program's by a relative error of at most 0.0051.
Values may be sent and summed in bfloat16 or wider, within the bound.
No kernel may reach another device: no remote copies, remote signals or barrier semaphores. Data moves between devices by JAX's collectives and lax.ppermute only.
A program may use at most 128 MiB of HBM per device.

v0:
```python
import jax
import jax.numpy as jnp
from jax import lax
from jax.sharding import PartitionSpec as P

WINDOW = 4096
QUERY_HEADS = 16
KEY_VALUE_HEADS = 4
HEAD_SIZE = 128


def from_behind(value, axis, steps):
    count = lax.axis_size(axis)
    first, last = (max(0, -steps), min(count, count - steps))
    return lax.ppermute(value, axis, [(source, source + steps) for source in range(first, last)])


def local(
    queries, key_matrix, value_matrix, attention_output, output_gradient, log_sum_norm, doc_ids
):
    count_of_rows = queries.shape[0]
    key_value_width = key_matrix.shape[1]
    query_width = queries.shape[1]
    group_width = QUERY_HEADS // KEY_VALUE_HEADS
    score_scale = HEAD_SIZE ** (-0.5)
    reach_shards = WINDOW // count_of_rows
    block_shards = max(1, min(512 // count_of_rows, reach_shards + 1))
    padded_shards = -(-(reach_shards + 1) // block_shards) * block_shards
    block_count = padded_shards // block_shards
    rows_per_block = block_shards * count_of_rows
    device = lax.axis_index("tok")
    doc_marks = doc_ids.astype(jnp.bfloat16)
    leap_plan = []
    shards_have = 1
    while shards_have < reach_shards + 1:
        shards_new = min(shards_have, reach_shards + 1 - shards_have)
        leap_plan.append((shards_have, shards_new))
        shards_have = shards_have + shards_new
    window_key = key_matrix[None]
    window_value = value_matrix[None]
    window_doc = doc_marks[None]
    for shards_have, shards_new in leap_plan:
        lower = shards_have - shards_new
        got_key, got_value, got_doc = from_behind(
            (window_key[lower:], window_value[lower:], window_doc[lower:]), "tok", shards_have
        )
        window_key = jnp.concatenate([got_key, window_key], 0)
        window_value = jnp.concatenate([got_value, window_value], 0)
        window_doc = jnp.concatenate([got_doc, window_doc], 0)
    front = padded_shards - reach_shards - 1
    window_key = jnp.pad(window_key, ((front, 0), (0, 0), (0, 0)))
    window_value = jnp.pad(window_value, ((front, 0), (0, 0), (0, 0)))
    window_doc = jnp.pad(window_doc, ((front, 0), (0, 0)))
    query_per_head = queries.reshape(count_of_rows, KEY_VALUE_HEADS, group_width, HEAD_SIZE)
    gradient_per_head = output_gradient.reshape(
        count_of_rows, KEY_VALUE_HEADS, group_width, HEAD_SIZE
    )
    dot_product_rows = output_gradient.astype(jnp.float32) * attention_output.astype(jnp.float32)
    delta_per_row = jnp.sum(
        dot_product_rows.reshape(count_of_rows, KEY_VALUE_HEADS, group_width, HEAD_SIZE), -1
    ).transpose(1, 2, 0)[..., None]
    norm_per_head = log_sum_norm.reshape(KEY_VALUE_HEADS, group_width, count_of_rows)[..., None]
    query_pos = device * count_of_rows + jnp.arange(count_of_rows, dtype=jnp.int32)
    key_first = (device - padded_shards + 1) * count_of_rows
    key_blocks = window_key.reshape(block_count, rows_per_block, key_value_width)
    value_blocks = window_value.reshape(block_count, rows_per_block, key_value_width)
    doc_blocks = window_doc.reshape(block_count, rows_per_block).astype(jnp.int32)

    def tile_terms(key_tile_rows, value_tile_rows, live_mask):
        key_per_head = key_tile_rows.reshape(rows_per_block, KEY_VALUE_HEADS, HEAD_SIZE)
        value_per_head = value_tile_rows.reshape(rows_per_block, KEY_VALUE_HEADS, HEAD_SIZE)
        scores = jnp.einsum(
            "tgrd,kgd->grtk", query_per_head, key_per_head, preferred_element_type=jnp.float32
        )
        attend = jnp.where(
            live_mask, jnp.exp(scores * score_scale - norm_per_head), jnp.float32(0.0)
        )
        dprob = jnp.einsum(
            "tgrd,kgd->grtk", gradient_per_head, value_per_head, preferred_element_type=jnp.float32
        )
        dscore = (attend * (dprob - delta_per_row) * score_scale).astype(jnp.bfloat16)
        attend_low = attend.astype(jnp.bfloat16)
        value_part = jnp.einsum(
            "grtk,tgrd->kgd", attend_low, gradient_per_head, preferred_element_type=jnp.float32
        ).reshape(rows_per_block, key_value_width)
        key_part = jnp.einsum(
            "grtk,tgrd->kgd", dscore, query_per_head, preferred_element_type=jnp.float32
        ).reshape(rows_per_block, key_value_width)
        query_part = jnp.einsum(
            "grtk,kgd->tgrd", dscore, key_per_head, preferred_element_type=jnp.float32
        ).reshape(count_of_rows, query_width)
        return (query_part, key_part, value_part)

    def block_step(query_total, inputs):
        key_tile_rows, value_tile_rows, key_docs, block_index = inputs
        key_pos = (
            key_first + block_index * rows_per_block + jnp.arange(rows_per_block, dtype=jnp.int32)
        )
        gap_rows = query_pos[:, None] - key_pos[None, :]
        live_mask = (
            (gap_rows >= 0)
            & (gap_rows < WINDOW)
            & (key_pos[None, :] >= 0)
            & (doc_ids[:, None] == key_docs[None, :])
        )
        terms = tile_terms(key_tile_rows, value_tile_rows, live_mask)
        return (query_total + terms[0], (terms[1], terms[2]))

    query_total, parts = lax.scan(
        block_step,
        jnp.zeros((count_of_rows, query_width), jnp.float32),
        (key_blocks, value_blocks, doc_blocks, jnp.arange(block_count, dtype=jnp.int32)),
    )
    key_parts = parts[0].reshape(padded_shards, count_of_rows, key_value_width)
    value_parts = parts[1].reshape(padded_shards, count_of_rows, key_value_width)
    base_index = padded_shards - 1 - reach_shards
    key_range = key_parts[base_index:]
    value_range = value_parts[base_index:]
    for shards_have, shards_new in reversed(leap_plan):
        got_key, got_value = from_behind(
            (key_range[:shards_new], value_range[:shards_new]), "tok", -shards_have
        )
        key_range = key_range[shards_new:].at[shards_have - shards_new :].add(got_key)
        value_range = value_range[shards_new:].at[shards_have - shards_new :].add(got_value)
    key_total = key_range[0]
    value_total = value_range[0]
    return (
        query_total.astype(jnp.bfloat16),
        key_total.astype(jnp.bfloat16),
        value_total.astype(jnp.bfloat16),
    )


def solution(mesh):
    return jax.shard_map(
        local,
        mesh=mesh,
        in_specs=(
            P(("groups", "tok"), None),
            P(("groups", "tok"), None),
            P(("groups", "tok"), None),
            P(("groups", "tok"), None),
            P(("groups", "tok"), None),
            P(None, ("groups", "tok")),
            P(("groups", "tok")),
        ),
        out_specs=(
            P(("groups", "tok"), None),
            P(("groups", "tok"), None),
            P(("groups", "tok"), None),
        ),
        check_vma=False,
    )
```

profile of v0, /device:TPU:5, one launch (start us, length us, event | category | flops | bytes accessed | tf_op | source)
XLA Modules:
  0.0 644.9 jit_solution(11860010224866137472)
XLA Ops:
  0.6 3.8 collective-permute-start.13
  7.7 3.1 collective-permute-start.14
  10.8 5.4 collective-permute-done.14
  17.2 3.2 collective-permute-start.15
  20.4 6.3 collective-permute-start.1
  26.7 5.8 collective-permute-done.1
  40.9 5.2 collective-permute-start.3
  46.0 24.7 %collective-permute-done.3 = bf16[4,128,512]{2,1,0:T(8,128)(2,1)S(1)} collective-permute-done((bf16[4,128,512]{2,1,0:T(8,128)(2,1)S(1)}, bf16[4,128,512]{2,1,0:T(8,128)(2,1)S(1)}, u32[]{:S(2)}, u32[]{:S(2)}) %collective-permute-start.3) | collective-permute-done | bytes 524320 | tf_op jit(solution)/shard_map/ppermute | solution.py:15
  71.0 28.6 %collective-permute-start.4 = (bf16[8,128,512]{2,1,0:T(8,128)(2,1)S(1)}, bf16[8,128,512]{2,1,0:T(8,128)(2,1)S(1)}, u32[]{:S(2)}, u32[]{:S(2)}) collective-permute-start(bf16[8,128,512]{2,1,0:T(8,128)(2,1)S(1)} %pad_maximum_fusion), channel_id=1, source_target_pairs={{0,8},{1,9},{2,10},{3,11},{4,12},{5,13},{6,14},{7,15},{16,24},{17,... | collective-permute-start | bytes 3145736 | tf_op jit(solution)/shard_map/ppermute | solution.py:15
  105.6 10.6 %collective-permute-done.4 = bf16[8,128,512]{2,1,0:T(8,128)(2,1)S(1)} collective-permute-done((bf16[8,128,512]{2,1,0:T(8,128)(2,1)S(1)}, bf16[8,128,512]{2,1,0:T(8,128)(2,1)S(1)}, u32[]{:S(2)}, u32[]{:S(2)}) %collective-permute-start.4) | collective-permute-done | bytes 1048608 | tf_op jit(solution)/shard_map/ppermute | solution.py:15
  123.3 28.7 %collective-permute-start.7 = (bf16[1,128]{1,0:T(2,128)(2,1)S(1)}, bf16[1,128]{1,0:T(2,128)(2,1)S(1)}, u32[]{:S(2)}, u32[]{:S(2)}) collective-permute-start(bf16[1,128]{1,0:T(2,128)(2,1)S(1)} %convert_bitcast_fusion), channel_id=1, source_target_pairs={{0,1},{1,2},{2,3},{3,4},{4,5},{5,6},{6,7},{7,8},{8,9},{9,10},{10,1... | collective-permute-start | bytes 776 | tf_op jit(solution)/shard_map/ppermute | solution.py:15
  152.6 4.5 collective-permute-start.8
  161.1 6.1 collective-permute-start.10
  185.1 3.5 concatenate.90
  201.9 104.1 %while.37 = (s32[]{:T(128)}, f32[128,2048]{0,1:T(8,128)S(1)}, f32[9,512,512]{1,2,0:T(8,128)}, f32[9,512,512]{1,2,0:T(8,128)}, bf16[9,512,512]{2,1,0:T(8,128)(2,1...) while((s32[]{:T(128)}, f32[128,2048]{0,1:T(8,128)S(1)}, ...), condition=%wide.region_2.3_spmd.clone, body=%wide.region_1.2_spmd.clone.sunk | while | flops 1354696320 | bytes 39555856 | solution.py:109
  306.1 9.6 %copy.69 = f32[9,512,512]{2,1,0:T(8,128)} copy(f32[9,512,512]{1,2,0:T(8,128)} %get-tuple-element.308) | data formatting | bytes 18874368 | tf_op jit(solution)/shard_map/while | solution.py:109
  317.4 7.8 %slice.336 = f32[8,512,512]{1,2,0:T(8,128)} slice(f32[9,512,512]{1,2,0:T(8,128)} %get-tuple-element.308), slice={[1:9], [0:512], [0:512]} | slice | bytes 16777216 | tf_op jit(solution)/shard_map/slice | solution.py:124
  325.2 9.2 %copy.68 = f32[8,512,512]{2,1,0:T(8,128)} copy(f32[8,512,512]{1,2,0:T(8,128)} %slice.336) | data formatting | bytes 16777216 | tf_op jit(solution)/shard_map/slice | solution.py:124
  336.1 4.9 slice.365
  343.6 9.6 %copy.67 = f32[9,512,512]{2,1,0:T(8,128)} copy(f32[9,512,512]{1,2,0:T(8,128)} %get-tuple-element.307) | data formatting | bytes 18874368 | tf_op jit(solution)/shard_map/while | solution.py:109
  354.8 7.7 %slice.322 = f32[8,512,512]{1,2,0:T(8,128)} slice(f32[9,512,512]{1,2,0:T(8,128)} %get-tuple-element.307), slice={[1:9], [0:512], [0:512]} | slice | bytes 16777216 | tf_op jit(solution)/shard_map/slice | solution.py:123
  362.5 9.2 %copy.66 = f32[8,512,512]{2,1,0:T(8,128)} copy(f32[8,512,512]{1,2,0:T(8,128)} %slice.322) | data formatting | bytes 16777216 | tf_op jit(solution)/shard_map/slice | solution.py:123
  377.3 4.6 slice_add_fusion
  386.1 135.9 %collective-permute-done.26 = f32[8,128,512]{2,1,0:T(8,128)S(1)} collective-permute-done((f32[8,128,512]{2,1,0:T(8,128)S(1)}, f32[8,128,512]{2,1,0:T(8,128)S(1)}, u32[]{:S(2)}, u32[]{:S(2)}) %collective-permute-start.26) | collective-permute-done | bytes 2097184 | tf_op jit(solution)/shard_map/ppermute | solution.py:15
  523.9 43.1 %collective-permute-done.20 = f32[8,128,512]{2,1,0:T(8,128)S(1)} collective-permute-done((f32[8,128,512]{2,1,0:T(8,128)S(1)}, f32[8,128,512]{2,1,0:T(8,128)S(1)}, u32[]{:S(2)}, u32[]{:S(2)}) %collective-permute-start.20) | collective-permute-done | bytes 2097184 | tf_op jit(solution)/shard_map/ppermute | solution.py:15
  568.8 20.9 %collective-permute-done.27 = f32[4,128,512]{2,1,0:T(8,128)S(1)} collective-permute-done((f32[4,128,512]{2,1,0:T(8,128)S(1)}, f32[4,128,512]{2,1,0:T(8,128)S(1)}, u32[]{:S(2)}, u32[]{:S(2)}) %collective-permute-start.27) | collective-permute-done | bytes 1048608 | tf_op jit(solution)/shard_map/ppermute | solution.py:15
  590.0 3.1 collective-permute-start.28
  593.1 19.1 %collective-permute-done.21 = f32[4,128,512]{2,1,0:T(8,128)S(1)} collective-permute-done((f32[4,128,512]{2,1,0:T(8,128)S(1)}, f32[4,128,512]{2,1,0:T(8,128)S(1)}, u32[]{:S(2)}, u32[]{:S(2)}) %collective-permute-start.21) | collective-permute-done | bytes 1048608 | tf_op jit(solution)/shard_map/ppermute | solution.py:15
  612.4 3.1 collective-permute-start.22
  615.5 8.8 %collective-permute-done.28 = f32[2,128,512]{2,1,0:T(8,128)S(1)} collective-permute-done((f32[2,128,512]{2,1,0:T(8,128)S(1)}, f32[2,128,512]{2,1,0:T(8,128)S(1)}, u32[]{:S(2)}, u32[]{:S(2)}) %collective-permute-start.28) | collective-permute-done | bytes 524320 | tf_op jit(solution)/shard_map/ppermute | solution.py:15
  626.9 8.6 %collective-permute-done.22 = f32[2,128,512]{2,1,0:T(8,128)S(1)} collective-permute-done((f32[2,128,512]{2,1,0:T(8,128)S(1)}, f32[2,128,512]{2,1,0:T(8,128)S(1)}, u32[]{:S(2)}, u32[]{:S(2)}) %collective-permute-start.22) | collective-permute-done | bytes 524320 | tf_op jit(solution)/shard_map/ppermute | solution.py:15
  639.8 4.5 collective-permute-done.23
  (320 shorter events, 187.9 us)
Async XLA Ops:
  0.6 6.1 collective-permute-start.13
  7.7 8.5 %collective-permute-start.14 = (bf16[2,128,512]{2,1,0:T(8,128)(2,1)S(1)}, bf16[2,128,512]{2,1,0:T(8,128)(2,1)S(1)}, u32[]{:S(2)}, u32[]{:S(2)}) collective-permute-start(bf16[2,128,512]{2,1,0:T(8,128)(2,1)S(1)} %pad_maximum_fusion.5), channel_id=1, source_target_pairs={{0,2},{1,3},{2,4},{3,5},{4,6},{5,7},{6,8},{7,9},{8,10},{9,11},{10,... | collective-permute-start | bytes 786440 | tf_op jit(solution)/shard_map/ppermute | solution.py:15
  17.2 18.4 %collective-permute-start.15 = (bf16[4,128,512]{2,1,0:T(8,128)(2,1)S(1)}, bf16[4,128,512]{2,1,0:T(8,128)(2,1)S(1)}, u32[]{:S(2)}, u32[]{:S(2)}) collective-permute-start(bf16[4,128,512]{2,1,0:T(8,128)(2,1)S(1)} %pad_maximum_fusion.3), channel_id=1, source_target_pairs={{0,4},{1,5},{2,6},{3,7},{4,8},{5,9},{6,10},{7,11},{8,12},{9,13},{1... | collective-permute-start | bytes 1572872 | tf_op jit(solution)/shard_map/ppermute | solution.py:15
  20.4 12.1 %collective-permute-start.1 = (bf16[1,128,512]{2,1,0:T(8,128)(2,1)}, bf16[1,128,512]{2,1,0:T(8,128)(2,1)S(1)}, u32[]{:S(2)}, u32[]{:S(2)}) collective-permute-start(bf16[1,128,512]{2,1,0:T(8,128)(2,1)} %bitcast.146), channel_id=1, source_target_pairs={{0,1},{1,2},{2,3},{3,4},{4,5},{5,6},{6,7},{7,8},{8,9},{9,10},{10,1... | collective-permute-start | bytes 393224 | tf_op jit(solution)/shard_map/ppermute | solution.py:15
  32.5 87.4 %copy-start.6 = (bf16[1,128,512]{2,1,0:T(8,128)(2,1)}, bf16[1,128,512]{2,1,0:T(8,128)(2,1)S(1)}, u32[]{:S(2)}) copy-start(bf16[1,128,512]{2,1,0:T(8,128)(2,1)S(1)} %collective-permute-done.1) | copy-start | bytes 393220
  33.5 7.3 %collective-permute-start.2 = (bf16[2,128,512]{2,1,0:T(8,128)(2,1)S(1)}, bf16[2,128,512]{2,1,0:T(8,128)(2,1)S(1)}, u32[]{:S(2)}, u32[]{:S(2)}) collective-permute-start(bf16[2,128,512]{2,1,0:T(8,128)(2,1)S(1)} %pad_maximum_fusion.4), channel_id=1, source_target_pairs={{0,2},{1,3},{2,4},{3,5},{4,6},{5,7},{6,8},{7,9},{8,10},{9,11},{10,... | collective-permute-start | bytes 786440 | tf_op jit(solution)/shard_map/ppermute | solution.py:15
  36.6 62.9 %collective-permute-start.16 = (bf16[8,128,512]{2,1,0:T(8,128)(2,1)S(1)}, bf16[8,128,512]{2,1,0:T(8,128)(2,1)S(1)}, u32[]{:S(2)}, u32[]{:S(2)}) collective-permute-start(bf16[8,128,512]{2,1,0:T(8,128)(2,1)S(1)} %pad_maximum_fusion.1), channel_id=1, source_target_pairs={{0,8},{1,9},{2,10},{3,11},{4,12},{5,13},{6,14},{7,15},{16,24},{17,... | collective-permute-start | bytes 3145736 | tf_op jit(solution)/shard_map/ppermute | solution.py:15
  40.9 29.9 %collective-permute-start.3 = (bf16[4,128,512]{2,1,0:T(8,128)(2,1)S(1)}, bf16[4,128,512]{2,1,0:T(8,128)(2,1)S(1)}, u32[]{:S(2)}, u32[]{:S(2)}) collective-permute-start(bf16[4,128,512]{2,1,0:T(8,128)(2,1)S(1)} %pad_maximum_fusion.2), channel_id=1, source_target_pairs={{0,4},{1,5},{2,6},{3,7},{4,8},{5,9},{6,10},{7,11},{8,12},{9,13},{1... | collective-permute-start | bytes 1572872 | tf_op jit(solution)/shard_map/ppermute | solution.py:15
  70.9 101.2 %copy-start.8 = (bf16[128,2048]{1,0:T(8,128)(2,1)S(1)}, bf16[128,2048]{1,0:T(8,128)(2,1)}, u32[]{:S(2)}) copy-start(bf16[128,2048]{1,0:T(8,128)(2,1)} %param.57) | copy-start | bytes 1572868
  71.0 45.2 %collective-permute-start.4 = (bf16[8,128,512]{2,1,0:T(8,128)(2,1)S(1)}, bf16[8,128,512]{2,1,0:T(8,128)(2,1)S(1)}, u32[]{:S(2)}, u32[]{:S(2)}) collective-permute-start(bf16[8,128,512]{2,1,0:T(8,128)(2,1)S(1)} %pad_maximum_fusion), channel_id=1, source_target_pairs={{0,8},{1,9},{2,10},{3,11},{4,12},{5,13},{6,14},{7,15},{16,24},{17,... | collective-permute-start | bytes 3145736 | tf_op jit(solution)/shard_map/ppermute | solution.py:15
  103.6 88.9 %collective-permute-start.17 = (bf16[16,128,512]{2,1,0:T(8,128)(2,1)}, bf16[16,128,512]{2,1,0:T(8,128)(2,1)}, u32[]{:S(2)}, u32[]{:S(2)}) collective-permute-start(bf16[16,128,512]{2,1,0:T(8,128)(2,1)} %constant_dynamic-update-slice_fusion.14), channel_id=1, source_target_pairs={} | collective-permute-start | bytes 6291464 | tf_op jit(solution)/shard_map/ppermute | solution.py:15
  121.2 73.2 %collective-permute-start.5 = (bf16[16,128,512]{2,1,0:T(8,128)(2,1)}, bf16[16,128,512]{2,1,0:T(8,128)(2,1)}, u32[]{:S(2)}, u32[]{:S(2)}) collective-permute-start(bf16[16,128,512]{2,1,0:T(8,128)(2,1)} %constant_dynamic-update-slice_fusion.2), channel_id=1, source_target_pairs={} | collective-permute-start | bytes 6291464 | tf_op jit(solution)/shard_map/ppermute | solution.py:15
  123.3 29.4 %collective-permute-start.7 = (bf16[1,128]{1,0:T(2,128)(2,1)S(1)}, bf16[1,128]{1,0:T(2,128)(2,1)S(1)}, u32[]{:S(2)}, u32[]{:S(2)}) collective-permute-start(bf16[1,128]{1,0:T(2,128)(2,1)S(1)} %convert_bitcast_fusion), channel_id=1, source_target_pairs={{0,1},{1,2},{2,3},{3,4},{4,5},{5,6},{6,7},{7,8},{8,9},{9,10},{10,1... | collective-permute-start | bytes 776 | tf_op jit(solution)/shard_map/ppermute | solution.py:15
  152.6 5.2 collective-permute-start.8
  157.9 3.2 collective-permute-start.9
  161.1 8.6 %collective-permute-start.10 = (bf16[8,128]{1,0:T(8,128)(2,1)S(1)}, bf16[8,128]{1,0:T(8,128)(2,1)S(1)}, u32[]{:S(2)}, u32[]{:S(2)}) collective-permute-start(bf16[8,128]{1,0:T(8,128)(2,1)S(1)} %pad_maximum_fusion.6), channel_id=1, source_target_pairs={{0,8},{1,9},{2,10},{3,11},{4,12},{5,13},{6,14},{7,15},{16,24},{17,... | collective-permute-start | bytes 6152 | tf_op jit(solution)/shard_map/ppermute | solution.py:15
  167.2 16.6 %collective-permute-start.6 = (bf16[1,128]{1,0:T(2,128)(2,1)S(1)}, bf16[1,128]{1,0:T(2,128)(2,1)}, u32[]{:S(2)}, u32[]{:S(2)}) collective-permute-start(bf16[1,128]{1,0:T(2,128)(2,1)S(1)} %convert_bitcast_fusion), channel_id=1, source_target_pairs={} | collective-permute-start | bytes 776 | tf_op jit(solution)/shard_map/ppermute | solution.py:15
  168.4 22.2 %collective-permute-start.12 = (bf16[1,128,512]{2,1,0:T(8,128)(2,1)S(1)}, bf16[1,128,512]{2,1,0:T(8,128)(2,1)}, u32[]{:S(2)}, u32[]{:S(2)}) collective-permute-start(bf16[1,128,512]{2,1,0:T(8,128)(2,1)S(1)} %bitcast.145), channel_id=1, source_target_pairs={} | collective-permute-start | bytes 393224 | tf_op jit(solution)/shard_map/ppermute | solution.py:15
  170.9 14.2 %collective-permute-start.11 = (bf16[16,128]{1,0:T(8,128)(2,1)}, bf16[16,128]{1,0:T(8,128)(2,1)}, u32[]{:S(2)}, u32[]{:S(2)}) collective-permute-start(bf16[16,128]{1,0:T(8,128)(2,1)} %concatenate.89), channel_id=1, source_target_pairs={} | collective-permute-start | bytes 12296 | tf_op jit(solution)/shard_map/ppermute | solution.py:15
  183.8 7.8 %collective-permute-start = (bf16[1,128,512]{2,1,0:T(8,128)(2,1)S(1)}, bf16[1,128,512]{2,1,0:T(8,128)(2,1)}, u32[]{:S(2)}, u32[]{:S(2)}) collective-permute-start(bf16[1,128,512]{2,1,0:T(8,128)(2,1)S(1)} %bitcast.150), channel_id=1, source_target_pairs={} | collective-permute-start | bytes 393224 | tf_op jit(solution)/shard_map/ppermute | solution.py:15
  316.6 17.8 %collective-permute-start.24 = (f32[1,128,512]{2,1,0:T(8,128)S(1)}, f32[1,128,512]{2,1,0:T(8,128)S(1)}, u32[]{:S(2)}, u32[]{:S(2)}) collective-permute-start(f32[1,128,512]{2,1,0:T(8,128)S(1)} %slice.363), channel_id=1, source_target_pairs={} | collective-permute-start | bytes 786440 | tf_op jit(solution)/shard_map/ppermute | solution.py:15
  340.9 36.4 %collective-permute-start.25 = (f32[16,128,512]{2,1,0:T(8,128)}, f32[16,128,512]{2,1,0:T(8,128)}, u32[]{:S(2)}, u32[]{:S(2)}) collective-permute-start(f32[16,128,512]{2,1,0:T(8,128)} %slice.365), channel_id=1, source_target_pairs={} | collective-permute-start | bytes 12582920 | tf_op jit(solution)/shard_map/ppermute | solution.py:15
  354.2 17.6 %collective-permute-start.18 = (f32[1,128,512]{2,1,0:T(8,128)S(1)}, f32[1,128,512]{2,1,0:T(8,128)S(1)}, u32[]{:S(2)}, u32[]{:S(2)}) collective-permute-start(f32[1,128,512]{2,1,0:T(8,128)S(1)} %slice.351), channel_id=1, source_target_pairs={} | collective-permute-start | bytes 786440 | tf_op jit(solution)/shard_map/ppermute | solution.py:15
  376.2 7.1 %collective-permute-start.19 = (f32[16,128,512]{2,1,0:T(8,128)S(1)}, f32[16,128,512]{2,1,0:T(8,128)S(1)}, u32[]{:S(2)}, u32[]{:S(2)}) collective-permute-start(f32[16,128,512]{2,1,0:T(8,128)S(1)} %slice.353), channel_id=1, source_target_pairs={} | collective-permute-start | bytes 12582920 | tf_op jit(solution)/shard_map/ppermute | solution.py:15
  382.1 139.9 %collective-permute-start.26 = (f32[8,128,512]{2,1,0:T(8,128)S(1)}, f32[8,128,512]{2,1,0:T(8,128)S(1)}, u32[]{:S(2)}, u32[]{:S(2)}) collective-permute-start(f32[8,128,512]{2,1,0:T(8,128)S(1)} %slice.367), channel_id=1, source_target_pairs={{8,0},{9,1},{10,2},{11,3},{12,4},{13,5},{14,6},{15,7},{24,16},{25,... | collective-permute-start | bytes 6291464 | tf_op jit(solution)/shard_map/ppermute | solution.py:15
  384.8 182.2 %collective-permute-start.20 = (f32[8,128,512]{2,1,0:T(8,128)S(1)}, f32[8,128,512]{2,1,0:T(8,128)S(1)}, u32[]{:S(2)}, u32[]{:S(2)}) collective-permute-start(f32[8,128,512]{2,1,0:T(8,128)S(1)} %slice.355), channel_id=1, source_target_pairs={{8,0},{9,1},{10,2},{11,3},{12,4},{13,5},{14,6},{15,7},{24,16},{25,... | collective-permute-start | bytes 6291464 | tf_op jit(solution)/shard_map/ppermute | solution.py:15
  522.6 67.1 %collective-permute-start.27 = (f32[4,128,512]{2,1,0:T(8,128)S(1)}, f32[4,128,512]{2,1,0:T(8,128)S(1)}, u32[]{:S(2)}, u32[]{:S(2)}) collective-permute-start(f32[4,128,512]{2,1,0:T(8,128)S(1)} %slice.369), channel_id=1, source_target_pairs={{4,0},{5,1},{6,2},{7,3},{8,4},{9,5},{10,6},{11,7},{12,8},{13,9},{1... | collective-permute-start | bytes 3145736 | tf_op jit(solution)/shard_map/ppermute | solution.py:15
  567.5 44.6 %collective-permute-start.21 = (f32[4,128,512]{2,1,0:T(8,128)S(1)}, f32[4,128,512]{2,1,0:T(8,128)S(1)}, u32[]{:S(2)}, u32[]{:S(2)}) collective-permute-start(f32[4,128,512]{2,1,0:T(8,128)S(1)} %slice.357), channel_id=1, source_target_pairs={{4,0},{5,1},{6,2},{7,3},{8,4},{9,5},{10,6},{11,7},{12,8},{13,9},{1... | collective-permute-start | bytes 3145736 | tf_op jit(solution)/shard_map/ppermute | solution.py:15
  590.0 34.4 %collective-permute-start.28 = (f32[2,128,512]{2,1,0:T(8,128)S(1)}, f32[2,128,512]{2,1,0:T(8,128)S(1)}, u32[]{:S(2)}, u32[]{:S(2)}) collective-permute-start(f32[2,128,512]{2,1,0:T(8,128)S(1)} %slice.371), channel_id=1, source_target_pairs={{2,0},{3,1},{4,2},{5,3},{6,4},{7,5},{8,6},{9,7},{10,8},{11,9},{12,... | collective-permute-start | bytes 1572872 | tf_op jit(solution)/shard_map/ppermute | solution.py:15
  612.4 23.1 %collective-permute-start.22 = (f32[2,128,512]{2,1,0:T(8,128)S(1)}, f32[2,128,512]{2,1,0:T(8,128)S(1)}, u32[]{:S(2)}, u32[]{:S(2)}) collective-permute-start(f32[2,128,512]{2,1,0:T(8,128)S(1)} %slice.359), channel_id=1, source_target_pairs={{2,0},{3,1},{4,2},{5,3},{6,4},{7,5},{8,6},{9,7},{10,8},{11,9},{12,... | collective-permute-start | bytes 1572872 | tf_op jit(solution)/shard_map/ppermute | solution.py:15
  624.4 14.6 %collective-permute-start.29 = (f32[1,128,512]{2,1,0:T(8,128)S(1)}, f32[1,128,512]{2,1,0:T(8,128)S(1)}, u32[]{:S(2)}, u32[]{:S(2)}) collective-permute-start(f32[1,128,512]{2,1,0:T(8,128)S(1)} %slice.373), channel_id=1, source_target_pairs={{1,0},{2,1},{3,2},{4,3},{5,4},{6,5},{7,6},{8,7},{9,8},{10,9},{11,1... | collective-permute-start | bytes 786440 | tf_op jit(solution)/shard_map/ppermute | solution.py:15
  635.7 8.6 %collective-permute-start.23 = (f32[1,128,512]{2,1,0:T(8,128)S(1)}, f32[1,128,512]{2,1,0:T(8,128)S(1)}, u32[]{:S(2)}, u32[]{:S(2)}) collective-permute-start(f32[1,128,512]{2,1,0:T(8,128)S(1)} %slice.361), channel_id=1, source_target_pairs={{1,0},{2,1},{3,2},{4,3},{5,4},{6,5},{7,6},{8,7},{9,8},{10,9},{11,1... | collective-permute-start | bytes 786440 | tf_op jit(solution)/shard_map/ppermute | solution.py:15
  (26 other events, 363.6 us)
where the time goes:
time: 649 us; the launch traced here: 645 us
  waiting for transfers between devices  293 us (45%)
  local copies, waits for them, and re-layouts  149 us (23%)
  starting transfers between devices  127 us (20%)
  matrix products  41.3 us (6%)
  other arithmetic  26.1 us (4%)
  loops' own time  6.72 us (1%)
    ppermute x30, waiting for transfers between devices, from_behind(): lax.ppermute(value, axis, [(source, source + steps) for source in range(f...  293 us
    ppermute x30, starting transfers between devices, from_behind(): lax.ppermute(value, axis, [(source, source + steps) for source in range(f...  127 us
    dynamic_slice x54, local copies, waits for them, and re-layouts, local(): lax.scan(block_step, jnp.zeros((count_of_rows, query_width), jnp.float32)...  35.1 us
    while x3, local copies, waits for them, and re-layouts, local(): lax.scan(block_step, jnp.zeros((count_of_rows, query_width), jnp.float32)...  20.1 us
    unnamed x61, local copies, waits for them, and re-layouts  17.6 us
    slice x2, local copies, waits for them, and re-layouts, local(): value_range[shards_new:].at[shards_have - shards_new:].add(got_value)  16.9 us
    slice x2, local copies, waits for them, and re-layouts, local(): key_range[shards_new:].at[shards_have - shards_new:].add(got_key)  16.9 us
    dot_general x9, matrix products, tile_terms(): jnp.einsum('tgrd,kgd->grtk', gradient_per_head, value_per_head, preferred...  14.4 us
  transfers between devices with their start and end apart: 30, of which 16 were waited for; matrix products, arithmetic and copies ran while one was open for 14% of the time, Pallas kernels for 0%

commit v1 on v0

v1 whole, which is shorter than its diff:
```python
import functools
import math

import jax
import jax.numpy as jnp
from jax import lax
from jax.experimental import pallas as pl
from jax.experimental.pallas import tpu as pltpu
from jax.sharding import PartitionSpec as P

WINDOW = 4096
QUERY_HEADS = 16
KEY_VALUE_HEADS = 4
HEAD_SIZE = 128
GROUP = QUERY_HEADS // KEY_VALUE_HEADS
SCALE = HEAD_SIZE ** (-0.5)
LOG2E = math.log2(math.e)
EXTRA = 8
F32 = jnp.float32
BF16 = jnp.bfloat16

VMEM = pl.BlockSpec(memory_space=pltpu.VMEM)
SMEM = pl.BlockSpec(memory_space=pltpu.SMEM)


def dot(a, b, dims):
    return lax.dot_general(a, b, (dims, ((), ())), preferred_element_type=F32)


def call(kernel, ins, outs, scratch=(), flops=0, name=None):
    size = sum(math.prod(o.shape) * o.dtype.itemsize for o in outs)
    size += sum(math.prod(x.shape) * x.dtype.itemsize for x in ins)
    return pl.pallas_call(
        kernel,
        out_shape=outs,
        in_specs=[SMEM] + [VMEM] * (len(ins) - 1),
        out_specs=[VMEM] * len(outs),
        scratch_shapes=list(scratch),
        cost_estimate=pl.CostEstimate(flops=flops, bytes_accessed=size, transcendentals=0),
        compiler_params=pltpu.CompilerParams(vmem_limit_bytes=48 << 20),
        name=name,
    )(*ins)


def pack_keys(rows, place, key_ref, value_ref, doc_ref, *outs):
    docs = jnp.broadcast_to((doc_ref[...] + 1).astype(F32), (EXTRA, rows)).astype(BF16)
    for s, out in enumerate(outs):
        cut = pl.ds(pl.multiple_of((place[1] ^ s) * HEAD_SIZE, HEAD_SIZE), HEAD_SIZE)
        out[0:rows, 0:HEAD_SIZE] = key_ref[:, cut]
        out[0:rows, HEAD_SIZE:] = value_ref[:, cut]
        out[rows:, 0:rows] = docs


def pack_queries(rows, place, query_ref, grad_ref, output_ref, norm_ref, *rest):
    outs, stats = rest[:-1], rest[-1]
    lane = lax.broadcasted_iota(jnp.int32, (rows, HEAD_SIZE), 1)
    columns = jnp.zeros((rows, HEAD_SIZE), F32)
    for h in range(QUERY_HEADS):
        cut = slice(h * HEAD_SIZE, (h + 1) * HEAD_SIZE)
        product = grad_ref[:, cut].astype(F32) * output_ref[:, cut].astype(F32)
        columns = jnp.where(lane == h, jnp.sum(product, 1, keepdims=True), columns)
    delta = columns.T
    for g in range(KEY_VALUE_HEADS):
        stats[g, 0:GROUP, :] = norm_ref[g * GROUP : (g + 1) * GROUP, :]
        stats[g, GROUP : 2 * GROUP, :] = delta[g * GROUP : (g + 1) * GROUP, :]
    width = GROUP * HEAD_SIZE
    for s, out in enumerate(outs):
        g = place[1] ^ s
        cut = pl.ds(pl.multiple_of(g * width, width), width)
        out[0:rows, 0:width] = query_ref[:, cut]
        out[0:rows, width:] = grad_ref[:, cut]
        left = stats[g]
        for part in range(3):
            term = left.astype(BF16)
            out[rows:, part * rows : (part + 1) * rows] = term
            left = left - term.astype(F32)


def join(rows, place, *refs):
    pieces, out = refs[:-1], refs[-1]
    block = rows + EXTRA
    for s, piece in enumerate(pieces):
        out[place[1] ^ s] = piece[...]


def attend(rows, offsets, reach, first, last, place, *refs):
    parts = KEY_VALUE_HEADS
    queries, refs = refs[:parts], refs[parts:]
    own, refs = refs[0], refs[1:]
    keys, refs = refs[: len(offsets)], refs[len(offsets) :]
    if not first:
        dq_in, refs = refs[0], refs[1:]
    if last:
        dq_out, refs = refs[:parts], refs[parts:]
    else:
        dq_out, refs = refs[0], refs[1:]
    kv_out, refs = refs[: len(offsets)], refs[len(offsets) :]
    stack_q, stack_g, stats, dq, dkv = refs
    row, me = place[0], place[1]
    width = GROUP * HEAD_SIZE
    span = parts * rows
    for s in range(parts):
        for h in range(GROUP):
            cut = slice(h * HEAD_SIZE, (h + 1) * HEAD_SIZE)
            stack_q[s, h * rows : (h + 1) * rows, :] = queries[s][0:rows, cut]
            cut = slice(width + h * HEAD_SIZE, width + (h + 1) * HEAD_SIZE)
            stack_g[s, h * rows : (h + 1) * rows, :] = queries[s][0:rows, cut]
        total = queries[s][rows:, 0:rows].astype(F32)
        total = total + queries[s][rows:, rows : 2 * rows].astype(F32)
        total = total + queries[s][rows:, 2 * rows : 3 * rows].astype(F32)
        stats[s] = total
    if first:
        dq[...] = jnp.zeros_like(dq)
    else:
        dq[...] = dq_in[...]
    for at, offset in enumerate(offsets):
        dkv[...] = jnp.zeros_like(dkv)

        def key_block(b, carry, at=at, offset=offset):
            key_rows = keys[at][b]
            key = key_rows[0:rows, 0:HEAD_SIZE]
            value = key_rows[0:rows, HEAD_SIZE:]
            key_docs = jnp.broadcast_to(key_rows[rows : rows + 1, 0:rows].astype(F32), (rows, rows)).T
            for s in range(parts):
                a = me ^ s
                near = offset * span + (a - b) * rows
                live = (near + rows - 1 >= 0) & (near - rows + 1 < reach) & (row >= offset)

                @pl.when(live)
                def _():
                    docs = own[a, rows : rows + 1, 0:rows].astype(F32)
                    gap = (
                        near
                        + lax.broadcasted_iota(jnp.int32, (rows, rows), 1)
                        - lax.broadcasted_iota(jnp.int32, (rows, rows), 0)
                    )
                    mask = key_docs == docs
                    if offset == 0:
                        mask = mask & (gap >= 0)
                    if (offset + 1) * span > WINDOW:
                        mask = mask & (gap < WINDOW)
                    query = stack_q[s]
                    grad = stack_g[s]
                    scores = dot(key, query, ((1,), (1,)))
                    dprob = dot(value, grad, ((1,), (1,)))
                    probs, dscores = [], []
                    for h in range(GROUP):
                        cut = slice(h * rows, (h + 1) * rows)
                        norm = stats[s, h : h + 1, :] * LOG2E
                        delta = stats[s, GROUP + h : GROUP + h + 1, :]
                        prob = jnp.exp2(scores[:, cut] * (SCALE * LOG2E) - norm)
                        prob = jnp.where(mask, prob, 0.0)
                        probs.append(prob.astype(BF16))
                        dscores.append((prob * (dprob[:, cut] - delta) * SCALE).astype(BF16))
                    prob = jnp.concatenate(probs, 1)
                    dscore = jnp.concatenate(dscores, 1)
                    dkv[b, :, 0:HEAD_SIZE] += dot(dscore, query, ((1,), (0,)))
                    dkv[b, :, HEAD_SIZE:] += dot(prob, grad, ((1,), (0,)))
                    dq[s] += dot(dscore, key, ((0,), (0,)))

            return carry

        lax.fori_loop(0, parts, key_block, 0)
        kv_out[at][...] = dkv[...].astype(kv_out[at].dtype)
    if last:
        for s in range(parts):
            for h in range(GROUP):
                cut = slice(h * HEAD_SIZE, (h + 1) * HEAD_SIZE)
                dq_out[s][:, cut] = dq[s, h * rows : (h + 1) * rows, :].astype(BF16)
    else:
        dq_out[...] = dq[...]


def add_terms(place, *refs):
    parts = KEY_VALUE_HEADS
    terms, outs = refs[:-parts], refs[-parts:]
    for s, out in enumerate(outs):
        b = place[1] ^ s
        total = terms[0][b]
        for term in terms[1:]:
            total = total + term[b].astype(F32)
        out[...] = total.astype(BF16)


def spread(place, *refs):
    parts = KEY_VALUE_HEADS
    pieces, outs = refs[:parts], refs[parts:]
    width = pieces[0].shape[1] // len(outs)
    for s, piece in enumerate(pieces):
        cut = pl.ds(pl.multiple_of((place[1] ^ s) * width, width), width)
        for k, out in enumerate(outs):
            out[:, cut] = piece[:, k * width : (k + 1) * width]


def local(
    queries, key_matrix, value_matrix, attention_output, output_gradient, log_sum_norm, doc_ids
):
    parts = KEY_VALUE_HEADS
    rows = queries.shape[0]
    count = lax.axis_size("tok")
    span = parts * rows
    reach = min(WINDOW, count * rows // 2)
    behind = min(-(-(reach - 1) // span), count // parts - 1)
    device = lax.axis_index("tok")
    place = jnp.stack([device // parts, device % parts]).astype(jnp.int32)
    width = GROUP * HEAD_SIZE
    shape = jax.ShapeDtypeStruct

    def across(value, s):
        return lax.ppermute(value, "tok", [(t, t ^ s) for t in range(count)])

    def along(value, steps):
        pairs = [(t, t + steps * parts) for t in range(count)]
        return lax.ppermute(value, "tok", [(a, b) for a, b in pairs if 0 <= b < count])

    def exchange(pieces):
        return [pieces[0]] + [across(pieces[s], s) for s in range(1, parts)]

    block = rows + EXTRA
    pieces = call(
        functools.partial(pack_keys, rows),
        (place, key_matrix, value_matrix, doc_ids.reshape(1, rows)),
        [shape((block, 2 * HEAD_SIZE), BF16)] * parts,
        name="pack_keys",
    )
    pieces = exchange(pieces)
    (own,) = call(
        functools.partial(join, rows),
        (place, *pieces),
        [shape((parts, block, 2 * HEAD_SIZE), BF16)],
        name="join",
    )
    query_pieces = call(
        functools.partial(pack_queries, rows),
        (place, queries, output_gradient, attention_output, log_sum_norm),
        [shape((block, 2 * width), BF16)] * parts,
        scratch=[pltpu.VMEM((parts, 2 * GROUP, rows), F32)],
        name="pack_queries",
    )
    query_pieces = exchange(query_pieces)
    windows = [own]
    for _ in range(behind):
        windows.append(along(windows[-1], 1))

    kv_shape = (parts, rows, 2 * HEAD_SIZE)
    stages = [tuple(range(min(2, behind + 1)))] + [(d,) for d in range(2, behind + 1)]
    dq, terms = None, []
    for k, offsets in enumerate(stages):
        first, last = k == 0, k == len(stages) - 1
        ins = [place, *query_pieces, own, *[windows[d] for d in offsets]]
        if not first:
            ins.append(dq)
        if last:
            outs = [shape((rows, width), BF16)] * parts
        else:
            outs = [shape((parts, GROUP * rows, HEAD_SIZE), F32)]
        outs = outs + [shape(kv_shape, F32 if d == 0 else BF16) for d in offsets]
        got = call(
            functools.partial(attend, rows, offsets, reach, first, last),
            ins,
            outs,
            scratch=[
                pltpu.VMEM((parts, GROUP * rows, HEAD_SIZE), BF16),
                pltpu.VMEM((parts, GROUP * rows, HEAD_SIZE), BF16),
                pltpu.VMEM((parts, 2 * GROUP, rows), F32),
                pltpu.VMEM((parts, GROUP * rows, HEAD_SIZE), F32),
                pltpu.VMEM(kv_shape, F32),
            ],
            flops=10 * len(offsets) * span * span * GROUP * HEAD_SIZE,
            name="attend_" + "_".join(map(str, offsets)),
        )
        dq = got[:parts] if last else got[0]
        for d, term in zip(offsets, got[-len(offsets) :]):
            terms.append(term if d == 0 else along(term, -d))

    (query_grad,) = call(
        spread, (place, *exchange(dq)), [shape((rows, parts * width), BF16)], name="spread_queries"
    )
    pieces = call(
        add_terms, (place, *terms), [shape((rows, 2 * HEAD_SIZE), BF16)] * parts, name="add_terms"
    )
    key_grad, value_grad = call(
        spread,
        (place, *exchange(pieces)),
        [shape((rows, parts * HEAD_SIZE), BF16)] * 2,
        name="spread_keys",
    )
    return query_grad, key_grad, value_grad


def solution(mesh):
    axes = ("groups", "tok")
    return jax.shard_map(
        local,
        mesh=mesh,
        in_specs=(
            P(axes, None),
            P(axes, None),
            P(axes, None),
            P(axes, None),
            P(axes, None),
            P(None, axes),
            P(axes),
        ),
        out_specs=(P(axes, None), P(axes, None), P(axes, None)),
        check_vma=False,
    )
```

time: 649 us -> 79 us (0.12)
  the two profiles are of different devices: /device:TPU:5 before, /device:TPU:0 now
where the time goes in v1:
time: 79 us; the launch traced here: 78.7 us
  waiting for transfers between devices  40.5 us (51%)
  starting transfers between devices  19.4 us (25%)
  Pallas kernels  13.3 us (17%)
  local copies, waits for them, and re-layouts  4.6 us (6%)
  between operations  0.81 us (1%)
    ppermute x4, waiting for transfers between devices, along(): lax.ppermute(value, 'tok', [(a, b) for a, b in pairs if 0 <= b < count])  26.8 us
    ppermute x12, waiting for transfers between devices, across(): return lax.ppermute(value, 'tok', [(t, t ^ s) for t in range(count)])  13.6 us
    pallas_call x8, Pallas kernels, call(): pl.pallas_call(kernel, out_shape=outs, in_specs=[SMEM] + [VMEM] * (len(in...  13.3 us
    ppermute x4, starting transfers between devices, along(): lax.ppermute(value, 'tok', [(a, b) for a, b in pairs if 0 <= b < count])  10.5 us
    ppermute x12, starting transfers between devices, across(): return lax.ppermute(value, 'tok', [(t, t ^ s) for t in range(count)])  8.94 us
    unnamed x14, local copies, waits for them, and re-layouts  4.6 us
  transfers between devices with their start and end apart: 16, of which 9 were waited for; matrix products, arithmetic and copies ran while one was open for 0% of the time, Pallas kernels for 14%

profile of v1, /device:TPU:0, one launch (start us, length us, event | category | flops | bytes accessed | tf_op | source)
XLA Modules:
  0.0 78.7 jit_solution(3881682805355094258)
XLA Ops:
  0.7 1.0 %copy-done.3 = bf16[128,512]{1,0:T(8,128)(2,1)S(1)} copy-done((bf16[128,512]{1,0:T(8,128)(2,1)S(1)}, bf16[128,512]{1,0:T(8,128)(2,1)}, u32[]{:S(2)}) %copy-start.3) | copy-done | bytes 131096
  1.7 0.9 %copy-done.4 = bf16[128,512]{1,0:T(8,128)(2,1)S(1)} copy-done((bf16[128,512]{1,0:T(8,128)(2,1)S(1)}, bf16[128,512]{1,0:T(8,128)(2,1)}, u32[]{:S(2)}) %copy-start.4) | copy-done | bytes 131096
  2.6 0.7 copy-done.6
  3.3 0.6 pack_keys.1
  3.9 0.6 collective-permute-start.3
  4.4 2.6 %collective-permute-start.4 = (bf16[136,256]{1,0:T(8,128)(2,1)S(1)}, bf16[136,256]{1,0:T(8,128)(2,1)S(1)}, u32[]{:S(2)}, u32[]{:S(2)}) collective-permute-start(bf16[136,256]{1,0:T(8,128)(2,1)S(1)} %get-tuple-element.31), channel_id=1, source_target_pairs={{0,2},{1,3},{2,0},{3,1},{4,6},{5,7},{6,4},{7,5},{8,10},{9,11},{10,... | collective-permute-start | bytes 208904 | tf_op jit(solution)/shard_map/ppermute | solution.py:210
  7.0 2.7 %collective-permute-done.4.refs_2_ = bf16[136,256]{1,0:T(8,128)(2,1)S(1)} collective-permute-done((bf16[136,256]{1,0:T(8,128)(2,1)S(1)}, bf16[136,256]{1,0:T(8,128)(2,1)S(1)}, u32[]{:S(2)}, u32[]{:S(2)}) %collective-permute-start.4) | collective-permute-done | bytes 69664 | tf_op jit(solution)/shard_map/ppermute | solution.py:210
  9.8 1.4 %collective-permute-done.5.refs_3_ = bf16[136,256]{1,0:T(8,128)(2,1)S(1)} collective-permute-done((bf16[136,256]{1,0:T(8,128)(2,1)S(1)}, bf16[136,256]{1,0:T(8,128)(2,1)S(1)}, u32[]{:S(2)}, u32[]{:S(2)}) %collective-permute-start.5) | collective-permute-done | bytes 69664 | tf_op jit(solution)/shard_map/ppermute | solution.py:210
  11.1 0.6 join.1.refs_4_.refs_5_
  11.7 3.5 %collective-permute-start.6 = (bf16[4,136,256]{2,1,0:T(8,128)(2,1)S(1)}, bf16[4,136,256]{2,1,0:T(8,128)(2,1)S(1)}, u32[]{:S(2)}, u32[]{:S(2)}) collective-permute-start(bf16[4,136,256]{2,1,0:T(8,128)(2,1)S(1)} %join.1.refs_4_.refs_5_), channel_id=1, source_target_pairs={{0,4},{1,5},{2,6},{3,7},{4,8},{5,9},{6,10},{7,11},{8,12},{9,13},{1... | collective-permute-start | bytes 835592 | tf_op jit(solution)/shard_map/ppermute | solution.py:214
  15.3 1.0 %copy-done.1 = bf16[128,2048]{1,0:T(8,128)(2,1)S(1)} copy-done((bf16[128,2048]{1,0:T(8,128)(2,1)S(1)}, bf16[128,2048]{1,0:T(8,128)(2,1)}, u32[]{:S(2)}) %copy-start.1) | copy-done | bytes 524312
  16.3 1.0 %copy-done.2 = bf16[128,2048]{1,0:T(8,128)(2,1)S(1)} copy-done((bf16[128,2048]{1,0:T(8,128)(2,1)S(1)}, bf16[128,2048]{1,0:T(8,128)(2,1)}, u32[]{:S(2)}) %copy-start.2) | copy-done | bytes 524312
  17.3 0.9 %pack_queries.1 = (bf16[136,1024]{1,0:T(8,128)(2,1)S(1)}, bf16[136,1024]{1,0:T(8,128)(2,1)S(1)}, bf16[136,1024]{1,0:T(8,128)(2,1)S(1)}, bf16[136,1024]{1,0:T(8,128)(2,1)S(1)}) custom-call(s32[2]{0:T(128)S(1)} %pad_add_fusion.place, bf16[128,2048]{1,0:T(8,128)(2,1)S(1)} %copy-done, bf16[128,2048]{1,0:T(8,128)(2,1)S(1)} %copy-done.1, ...), custom_call_target="tpu_custom_call" | custom-call | bytes 2695176 | tf_op jit(solution)/shard_map/pack_queries/pallas_call | solution.py:33
  18.4 1.4 %collective-permute-start.1 = (bf16[136,1024]{1,0:T(8,128)(2,1)S(1)}, bf16[136,1024]{1,0:T(8,128)(2,1)S(1)}, u32[]{:S(2)}, u32[]{:S(2)}) collective-permute-start(bf16[136,1024]{1,0:T(8,128)(2,1)S(1)} %get-tuple-element.27), channel_id=1, source_target_pairs={{0,2},{1,3},{2,0},{3,1},{4,6},{5,7},{6,4},{7,5},{8,10},{9,11},{10,... | collective-permute-start | bytes 835592 | tf_op jit(solution)/shard_map/ppermute | solution.py:210
  20.2 1.2 %collective-permute-done.6.refs_6_ = bf16[4,136,256]{2,1,0:T(8,128)(2,1)S(1)} collective-permute-done((bf16[4,136,256]{2,1,0:T(8,128)(2,1)S(1)}, bf16[4,136,256]{2,1,0:T(8,128)(2,1)S(1)}, u32[]{:S(2)}, u32[]{:S(2)}) %collective-permute-start.6) | collective-permute-done | bytes 278560 | tf_op jit(solution)/shard_map/ppermute | solution.py:214
  21.4 4.4 %collective-permute-start.7 = (bf16[4,136,256]{2,1,0:T(8,128)(2,1)S(1)}, bf16[4,136,256]{2,1,0:T(8,128)(2,1)S(1)}, u32[]{:S(2)}, u32[]{:S(2)}) collective-permute-start(bf16[4,136,256]{2,1,0:T(8,128)(2,1)S(1)} %collective-permute-done.6.refs_6_), channel_id=1, source_target_pairs={{0,4},{1,5},{2,6},{3,7},{4,8},{5,9},{6,10},{7,11},{8,12},{9,13},{1... | collective-permute-start | bytes 835592 | tf_op jit(solution)/shard_map/ppermute | solution.py:214
  25.8 2.1 %collective-permute-done.1.refs_2_ = bf16[136,1024]{1,0:T(8,128)(2,1)S(1)} collective-permute-done((bf16[136,1024]{1,0:T(8,128)(2,1)S(1)}, bf16[136,1024]{1,0:T(8,128)(2,1)S(1)}, u32[]{:S(2)}, u32[]{:S(2)}) %collective-permute-start.1) | collective-permute-done | bytes 278560 | tf_op jit(solution)/shard_map/ppermute | solution.py:210
  28.0 4.9 %collective-permute-done.2.refs_3_ = bf16[136,1024]{1,0:T(8,128)(2,1)S(1)} collective-permute-done((bf16[136,1024]{1,0:T(8,128)(2,1)S(1)}, bf16[136,1024]{1,0:T(8,128)(2,1)S(1)}, u32[]{:S(2)}, u32[]{:S(2)}) %collective-permute-start.2) | collective-permute-done | bytes 278560 | tf_op jit(solution)/shard_map/ppermute | solution.py:210
  32.9 6.5 %attend_0_1.1 = (f32[4,512,128]{2,1,0:T(8,128)S(1)}, f32[4,128,256]{2,1,0:T(8,128)S(1)}, bf16[4,128,256]{2,1,0:T(8,128)(2,1)S(1)}) custom-call(s32[2]{0:T(128)S(1)} %pad_add_fusion.place, bf16[136,1024]{1,0:T(8,128)(2,1)S(1)} %get-tuple-element.25.refs_0_, bf16[136,1024]{1,0:T(8,128)(2,1)S(1)} %collective-permute-done.refs_1_, ...), custom_call_target="tpu_custom_call" | custom-call | flops 2684354560 | bytes 3784712 | tf_op jit(solution)/shard_map/attend_0_1/pallas_call | solution.py:33
  39.4 1.3 %collective-permute-start.11 = (bf16[4,128,256]{2,1,0:T(8,128)(2,1)S(1)}, bf16[4,128,256]{2,1,0:T(8,128)(2,1)S(1)}, u32[]{:S(2)}, u32[]{:S(2)}) collective-permute-start(bf16[4,128,256]{2,1,0:T(8,128)(2,1)S(1)} %get-tuple-element.39), channel_id=1, source_target_pairs={{4,0},{5,1},{6,2},{7,3},{8,4},{9,5},{10,6},{11,7},{12,8},{13,9},{1... | collective-permute-start | bytes 786440 | tf_op jit(solution)/shard_map/ppermute | solution.py:214
  40.7 1.4 %attend_2.1 = (bf16[128,512]{1,0:T(8,128)(2,1)S(1)}, bf16[128,512]{1,0:T(8,128)(2,1)S(1)}, bf16[128,512]{1,0:T(8,128)(2,1)S(1)}, bf16[128,512]{1,0:T(8,128)(2,1)S(1)}, bf16[4,128,256]{2,1,0:T(8,128)(2,1)S(1)}) custom-call(s32[2]{0:T(128)S(1)} %pad_add_fusion.place, bf16[136,1024]{1,0:T(8,128)(2,1)S(1)} %get-tuple-element.25.refs_0_, ...), custom_call_target="tpu_custom_call" | custom-call | flops 1342177280 | bytes 3506184 | tf_op jit(solution)/shard_map/attend_2/pallas_call | solution.py:33
  42.1 1.3 %collective-permute-start.12 = (bf16[4,128,256]{2,1,0:T(8,128)(2,1)S(1)}, bf16[4,128,256]{2,1,0:T(8,128)(2,1)S(1)}, u32[]{:S(2)}, u32[]{:S(2)}) collective-permute-start(bf16[4,128,256]{2,1,0:T(8,128)(2,1)S(1)} %get-tuple-element.40), channel_id=1, source_target_pairs={{8,0},{9,1},{10,2},{11,3},{12,4},{13,5},{14,6},{15,7},{24,16},{25,... | collective-permute-start | bytes 786440 | tf_op jit(solution)/shard_map/ppermute | solution.py:214
  43.8 1.3 %collective-permute-start.9 = (bf16[128,512]{1,0:T(8,128)(2,1)S(1)}, bf16[128,512]{1,0:T(8,128)(2,1)S(1)}, u32[]{:S(2)}, u32[]{:S(2)}) collective-permute-start(bf16[128,512]{1,0:T(8,128)(2,1)S(1)} %get-tuple-element.36), channel_id=1, source_target_pairs={{0,2},{1,3},{2,0},{3,1},{4,6},{5,7},{6,4},{7,5},{8,10},{9,11},{10,... | collective-permute-start | bytes 393224 | tf_op jit(solution)/shard_map/ppermute | solution.py:210
  45.3 11.6 %collective-permute-done.11.refs_1_ = bf16[4,128,256]{2,1,0:T(8,128)(2,1)S(1)} collective-permute-done((bf16[4,128,256]{2,1,0:T(8,128)(2,1)S(1)}, bf16[4,128,256]{2,1,0:T(8,128)(2,1)S(1)}, u32[]{:S(2)}, u32[]{:S(2)}) %collective-permute-start.11) | collective-permute-done | bytes 262176 | tf_op jit(solution)/shard_map/ppermute | solution.py:214
  56.9 14.1 %collective-permute-done.12.refs_2_ = bf16[4,128,256]{2,1,0:T(8,128)(2,1)S(1)} collective-permute-done((bf16[4,128,256]{2,1,0:T(8,128)(2,1)S(1)}, bf16[4,128,256]{2,1,0:T(8,128)(2,1)S(1)}, u32[]{:S(2)}, u32[]{:S(2)}) %collective-permute-start.12) | collective-permute-done | bytes 262176 | tf_op jit(solution)/shard_map/ppermute | solution.py:214
  71.0 0.6 add_terms.1
  71.7 1.3 %collective-permute-start.14 = (bf16[128,256]{1,0:T(8,128)(2,1)S(1)}, bf16[128,256]{1,0:T(8,128)(2,1)S(1)}, u32[]{:S(2)}, u32[]{:S(2)}) collective-permute-start(bf16[128,256]{1,0:T(8,128)(2,1)S(1)} %get-tuple-element.43), channel_id=1, source_target_pairs={{0,2},{1,3},{2,0},{3,1},{4,6},{5,7},{6,4},{7,5},{8,10},{9,11},{10,... | collective-permute-start | bytes 196616 | tf_op jit(solution)/shard_map/ppermute | solution.py:210
  73.0 0.5 collective-permute-start.15
  73.5 1.4 %spread_queries.1 = bf16[128,2048]{1,0:T(8,128)(2,1)} custom-call(s32[2]{0:T(128)S(1)} %pad_add_fusion.place, bf16[128,512]{1,0:T(8,128)(2,1)S(1)} %get-tuple-element.34.refs_0_, bf16[128,512]{1,0:T(8,128)(2,1)S(1)} %collective-permute-done.8.refs_1_, bf16[128,512]{1,0:T(8,128)(2,1)S(1)} %collective-permute-done.9.refs_2_, ...), custom_call_target="tpu_custom_call" | custom-call | bytes 1048584 | tf_op jit(solution)/shard_map/spread_queries/pallas_call | solution.py:33
  74.9 1.4 %collective-permute-done.14.refs_2_ = bf16[128,256]{1,0:T(8,128)(2,1)S(1)} collective-permute-done((bf16[128,256]{1,0:T(8,128)(2,1)S(1)}, bf16[128,256]{1,0:T(8,128)(2,1)S(1)}, u32[]{:S(2)}, u32[]{:S(2)}) %collective-permute-start.14) | collective-permute-done | bytes 65568 | tf_op jit(solution)/shard_map/ppermute | solution.py:210
  76.3 1.1 %collective-permute-done.15.refs_3_ = bf16[128,256]{1,0:T(8,128)(2,1)S(1)} collective-permute-done((bf16[128,256]{1,0:T(8,128)(2,1)S(1)}, bf16[128,256]{1,0:T(8,128)(2,1)S(1)}, u32[]{:S(2)}, u32[]{:S(2)}) %collective-permute-start.15) | collective-permute-done | bytes 65568 | tf_op jit(solution)/shard_map/ppermute | solution.py:210
  77.4 1.3 %spread_keys.1 = (bf16[128,512]{1,0:T(8,128)(2,1)}, bf16[128,512]{1,0:T(8,128)(2,1)}) custom-call(s32[2]{0:T(128)S(1)} %pad_add_fusion.place, bf16[128,256]{1,0:T(8,128)(2,1)S(1)} %get-tuple-element.41.refs_0_, bf16[128,256]{1,0:T(8,128)(2,1)S(1)} %collective-permute-done.13.refs_1_, bf16[128,256]{1,0:T(8,128)(2,1)S(1)} %collective-permute-done.14.refs_2_, ...), custom_call_target="tpu_custom_call" | custom-call | bytes 524296 | tf_op jit(solution)/shard_map/spread_keys/pallas_call | solution.py:33
  (23 shorter events, 1.4 us)
Async XLA Ops:
  0.6 14.6 %copy-start = (bf16[128,2048]{1,0:T(8,128)(2,1)S(1)}, bf16[128,2048]{1,0:T(8,128)(2,1)}, u32[]{:S(2)}) copy-start(bf16[128,2048]{1,0:T(8,128)(2,1)} %query_ref.1) | copy-start | bytes 1572868
  0.7 1.0 %copy-start.3 = (bf16[128,512]{1,0:T(8,128)(2,1)S(1)}, bf16[128,512]{1,0:T(8,128)(2,1)}, u32[]{:S(2)}) copy-start(bf16[128,512]{1,0:T(8,128)(2,1)} %key_ref.1) | copy-start | bytes 393220
  1.7 0.9 %copy-start.4 = (bf16[128,512]{1,0:T(8,128)(2,1)S(1)}, bf16[128,512]{1,0:T(8,128)(2,1)}, u32[]{:S(2)}) copy-start(bf16[128,512]{1,0:T(8,128)(2,1)} %value_ref.1) | copy-start | bytes 393220
  2.6 0.7 copy-start.6
  3.9 3.2 %collective-permute-start.3 = (bf16[136,256]{1,0:T(8,128)(2,1)S(1)}, bf16[136,256]{1,0:T(8,128)(2,1)S(1)}, u32[]{:S(2)}, u32[]{:S(2)}) collective-permute-start(bf16[136,256]{1,0:T(8,128)(2,1)S(1)} %get-tuple-element.30), channel_id=1, source_target_pairs={{0,1},{1,0},{2,3},{3,2},{4,5},{5,4},{6,7},{7,6},{8,9},{9,8},{10,11... | collective-permute-start | bytes 208904 | tf_op jit(solution)/shard_map/ppermute | solution.py:210
  4.4 5.4 %collective-permute-start.4 = (bf16[136,256]{1,0:T(8,128)(2,1)S(1)}, bf16[136,256]{1,0:T(8,128)(2,1)S(1)}, u32[]{:S(2)}, u32[]{:S(2)}) collective-permute-start(bf16[136,256]{1,0:T(8,128)(2,1)S(1)} %get-tuple-element.31), channel_id=1, source_target_pairs={{0,2},{1,3},{2,0},{3,1},{4,6},{5,7},{6,4},{7,5},{8,10},{9,11},{10,... | collective-permute-start | bytes 208904 | tf_op jit(solution)/shard_map/ppermute | solution.py:210
  7.0 4.1 %collective-permute-start.5 = (bf16[136,256]{1,0:T(8,128)(2,1)S(1)}, bf16[136,256]{1,0:T(8,128)(2,1)S(1)}, u32[]{:S(2)}, u32[]{:S(2)}) collective-permute-start(bf16[136,256]{1,0:T(8,128)(2,1)S(1)} %get-tuple-element.32), channel_id=1, source_target_pairs={{0,3},{1,2},{2,1},{3,0},{4,7},{5,6},{6,5},{7,4},{8,11},{9,10},{10,... | collective-permute-start | bytes 208904 | tf_op jit(solution)/shard_map/ppermute | solution.py:210
  11.1 4.1 %copy-start.5 = (f32[16,128]{1,0:T(8,128)S(1)}, f32[16,128]{1,0:T(8,128)}, u32[]{:S(2)}) copy-start(f32[16,128]{1,0:T(8,128)} %norm_ref.1) | copy-start | bytes 24580
  11.7 9.7 %collective-permute-start.6 = (bf16[4,136,256]{2,1,0:T(8,128)(2,1)S(1)}, bf16[4,136,256]{2,1,0:T(8,128)(2,1)S(1)}, u32[]{:S(2)}, u32[]{:S(2)}) collective-permute-start(bf16[4,136,256]{2,1,0:T(8,128)(2,1)S(1)} %join.1.refs_4_.refs_5_), channel_id=1, source_target_pairs={{0,4},{1,5},{2,6},{3,7},{4,8},{5,9},{6,10},{7,11},{8,12},{9,13},{1... | collective-permute-start | bytes 835592 | tf_op jit(solution)/shard_map/ppermute | solution.py:214
  15.3 1.0 %copy-start.1 = (bf16[128,2048]{1,0:T(8,128)(2,1)S(1)}, bf16[128,2048]{1,0:T(8,128)(2,1)}, u32[]{:S(2)}) copy-start(bf16[128,2048]{1,0:T(8,128)(2,1)} %grad_ref.1) | copy-start | bytes 1572868
  16.3 1.0 %copy-start.2 = (bf16[128,2048]{1,0:T(8,128)(2,1)S(1)}, bf16[128,2048]{1,0:T(8,128)(2,1)}, u32[]{:S(2)}) copy-start(bf16[128,2048]{1,0:T(8,128)(2,1)} %output_ref.1) | copy-start | bytes 1572868
  18.3 7.5 %collective-permute-start = (bf16[136,1024]{1,0:T(8,128)(2,1)S(1)}, bf16[136,1024]{1,0:T(8,128)(2,1)S(1)}, u32[]{:S(2)}, u32[]{:S(2)}) collective-permute-start(bf16[136,1024]{1,0:T(8,128)(2,1)S(1)} %get-tuple-element.26), channel_id=1, source_target_pairs={{0,1},{1,0},{2,3},{3,2},{4,5},{5,4},{6,7},{7,6},{8,9},{9,8},{10,11... | collective-permute-start | bytes 835592 | tf_op jit(solution)/shard_map/ppermute | solution.py:210
  18.4 9.6 %collective-permute-start.1 = (bf16[136,1024]{1,0:T(8,128)(2,1)S(1)}, bf16[136,1024]{1,0:T(8,128)(2,1)S(1)}, u32[]{:S(2)}, u32[]{:S(2)}) collective-permute-start(bf16[136,1024]{1,0:T(8,128)(2,1)S(1)} %get-tuple-element.27), channel_id=1, source_target_pairs={{0,2},{1,3},{2,0},{3,1},{4,6},{5,7},{6,4},{7,5},{8,10},{9,11},{10,... | collective-permute-start | bytes 835592 | tf_op jit(solution)/shard_map/ppermute | solution.py:210
  19.8 13.1 %collective-permute-start.2 = (bf16[136,1024]{1,0:T(8,128)(2,1)S(1)}, bf16[136,1024]{1,0:T(8,128)(2,1)S(1)}, u32[]{:S(2)}, u32[]{:S(2)}) collective-permute-start(bf16[136,1024]{1,0:T(8,128)(2,1)S(1)} %get-tuple-element.28), channel_id=1, source_target_pairs={{0,3},{1,2},{2,1},{3,0},{4,7},{5,6},{6,5},{7,4},{8,11},{9,10},{10,... | collective-permute-start | bytes 835592 | tf_op jit(solution)/shard_map/ppermute | solution.py:210
  21.4 19.2 %collective-permute-start.7 = (bf16[4,136,256]{2,1,0:T(8,128)(2,1)S(1)}, bf16[4,136,256]{2,1,0:T(8,128)(2,1)S(1)}, u32[]{:S(2)}, u32[]{:S(2)}) collective-permute-start(bf16[4,136,256]{2,1,0:T(8,128)(2,1)S(1)} %collective-permute-done.6.refs_6_), channel_id=1, source_target_pairs={{0,4},{1,5},{2,6},{3,7},{4,8},{5,9},{6,10},{7,11},{8,12},{9,13},{1... | collective-permute-start | bytes 835592 | tf_op jit(solution)/shard_map/ppermute | solution.py:214
  39.4 17.5 %collective-permute-start.11 = (bf16[4,128,256]{2,1,0:T(8,128)(2,1)S(1)}, bf16[4,128,256]{2,1,0:T(8,128)(2,1)S(1)}, u32[]{:S(2)}, u32[]{:S(2)}) collective-permute-start(bf16[4,128,256]{2,1,0:T(8,128)(2,1)S(1)} %get-tuple-element.39), channel_id=1, source_target_pairs={{4,0},{5,1},{6,2},{7,3},{8,4},{9,5},{10,6},{11,7},{12,8},{13,9},{1... | collective-permute-start | bytes 786440 | tf_op jit(solution)/shard_map/ppermute | solution.py:214
  42.1 28.9 %collective-permute-start.12 = (bf16[4,128,256]{2,1,0:T(8,128)(2,1)S(1)}, bf16[4,128,256]{2,1,0:T(8,128)(2,1)S(1)}, u32[]{:S(2)}, u32[]{:S(2)}) collective-permute-start(bf16[4,128,256]{2,1,0:T(8,128)(2,1)S(1)} %get-tuple-element.40), channel_id=1, source_target_pairs={{8,0},{9,1},{10,2},{11,3},{12,4},{13,5},{14,6},{15,7},{24,16},{25,... | collective-permute-start | bytes 786440 | tf_op jit(solution)/shard_map/ppermute | solution.py:214
  43.4 29.6 %collective-permute-start.8 = (bf16[128,512]{1,0:T(8,128)(2,1)S(1)}, bf16[128,512]{1,0:T(8,128)(2,1)S(1)}, u32[]{:S(2)}, u32[]{:S(2)}) collective-permute-start(bf16[128,512]{1,0:T(8,128)(2,1)S(1)} %get-tuple-element.35), channel_id=1, source_target_pairs={{0,1},{1,0},{2,3},{3,2},{4,5},{5,4},{6,7},{7,6},{8,9},{9,8},{10,11... | collective-permute-start | bytes 393224 | tf_op jit(solution)/shard_map/ppermute | solution.py:210
  43.8 29.7 %collective-permute-start.9 = (bf16[128,512]{1,0:T(8,128)(2,1)S(1)}, bf16[128,512]{1,0:T(8,128)(2,1)S(1)}, u32[]{:S(2)}, u32[]{:S(2)}) collective-permute-start(bf16[128,512]{1,0:T(8,128)(2,1)S(1)} %get-tuple-element.36), channel_id=1, source_target_pairs={{0,2},{1,3},{2,0},{3,1},{4,6},{5,7},{6,4},{7,5},{8,10},{9,11},{10,... | collective-permute-start | bytes 393224 | tf_op jit(solution)/shard_map/ppermute | solution.py:210
  45.2 28.4 %collective-permute-start.10 = (bf16[128,512]{1,0:T(8,128)(2,1)S(1)}, bf16[128,512]{1,0:T(8,128)(2,1)S(1)}, u32[]{:S(2)}, u32[]{:S(2)}) collective-permute-start(bf16[128,512]{1,0:T(8,128)(2,1)S(1)} %get-tuple-element.37), channel_id=1, source_target_pairs={{0,3},{1,2},{2,1},{3,0},{4,7},{5,6},{6,5},{7,4},{8,11},{9,10},{10,... | collective-permute-start | bytes 393224 | tf_op jit(solution)/shard_map/ppermute | solution.py:210
  71.6 3.3 %collective-permute-start.13 = (bf16[128,256]{1,0:T(8,128)(2,1)S(1)}, bf16[128,256]{1,0:T(8,128)(2,1)S(1)}, u32[]{:S(2)}, u32[]{:S(2)}) collective-permute-start(bf16[128,256]{1,0:T(8,128)(2,1)S(1)} %get-tuple-element.42), channel_id=1, source_target_pairs={{0,1},{1,0},{2,3},{3,2},{4,5},{5,4},{6,7},{7,6},{8,9},{9,8},{10,11... | collective-permute-start | bytes 196616 | tf_op jit(solution)/shard_map/ppermute | solution.py:210
  71.7 4.6 %collective-permute-start.14 = (bf16[128,256]{1,0:T(8,128)(2,1)S(1)}, bf16[128,256]{1,0:T(8,128)(2,1)S(1)}, u32[]{:S(2)}, u32[]{:S(2)}) collective-permute-start(bf16[128,256]{1,0:T(8,128)(2,1)S(1)} %get-tuple-element.43), channel_id=1, source_target_pairs={{0,2},{1,3},{2,0},{3,1},{4,6},{5,7},{6,4},{7,5},{8,10},{9,11},{10,... | collective-permute-start | bytes 196616 | tf_op jit(solution)/shard_map/ppermute | solution.py:210
  73.0 4.4 %collective-permute-start.15 = (bf16[128,256]{1,0:T(8,128)(2,1)S(1)}, bf16[128,256]{1,0:T(8,128)(2,1)S(1)}, u32[]{:S(2)}, u32[]{:S(2)}) collective-permute-start(bf16[128,256]{1,0:T(8,128)(2,1)S(1)} %get-tuple-element.44), channel_id=1, source_target_pairs={{0,3},{1,2},{2,1},{3,0},{4,7},{5,6},{6,5},{7,4},{8,11},{9,10},{10,... | collective-permute-start | bytes 196616 | tf_op jit(solution)/shard_map/ppermute | solution.py:210
